TPU v7x, 128 devices: a whole 4x4x4 slice. The times are simulated.
128 devices in a mesh: wide: 16 (over x_hi, z, core), narrow: 8 (over y, x_lo).
Axes of the slice: x: 4 (x_hi: 2, x_lo: 2; x = x_hi * 2 + x_lo), y: 4, z: 4, core: 2. Of those that a mesh axis runs over, the one named last changes fastest.
Arguments:
- block_states: bfloat16 [32, 64, 4096], P('wide', None, 'narrow'), may hold values from -6 to 6
- attn_gain: float32 [4096], replicated, may hold values from 0.1 to 1.9
- ffn_gain: float32 [4096], replicated, may hold values from 0.1 to 1.9
- final_gain: float32 [4096], replicated, may hold values from 0.1 to 1.9
- w_query: bfloat16 [4096, 4096], P(None, 'narrow'), may hold values from -0.09375 to 0.09375
- w_keyval: bfloat16 [4096, 1024], replicated, may hold values from -0.09375 to 0.09375
- w_out: bfloat16 [4096, 4096], P('narrow'), may hold values from -0.09375 to 0.09375
- w_gate: bfloat16 [4096, 1024], P(None, 'narrow'), may hold values from -0.09375 to 0.09375
- w_up: bfloat16 [4096, 1024], P(None, 'narrow'), may hold values from -0.09375 to 0.09375
- w_down: bfloat16 [1024, 4096], P('narrow'), may hold values from -0.1875 to 0.1875
- w_head: bfloat16 [4096, 131072], P(None, ('wide', 'narrow')), may hold values from -8 to 8
- cache: bfloat16 [32, 512, 4, 256], P('wide'), may hold values from -2000 to 2000
- prefix_lengths: int32 [32], P('wide'), may hold values from 128 to 512, as said below
- masked_positions: int32 [16, 64], replicated, may hold values from 0 to 63, as said below
Outputs:
- log_probs: float32 [1024, 131072], P(None, ('wide', 'narrow'))
- confidence: float32 [16, 64], replicated
Inputs may be any that keep to these rules, and one draw needn't show every extreme that they name: `prefix_lengths`: some request branch has exactly 512 valid positions. `masked_positions`: the 64 positions of one request are distinct.
All inputs are finite; a program needn't handle non-finite values.
Results may differ from a plain program's by a relative error of at most 0.024.
The roundings to bfloat16 on the way count: a program that leaves them out, or rounds other values in their place, can miss the bound.
Values may be sent and summed in bfloat16 or wider, within the bound.
No kernel may reach another device: no remote copies, remote signals or barrier semaphores. Data moves between devices by JAX's collectives and lax.ppermute only.
A program may use at most 128 MiB of HBM per device.

v0:
```python
import math
import jax
import jax.numpy as jnp
from jax import lax
from jax.sharding import PartitionSpec as P

KVH = 4
HD = 128
EPS = 1e-06
GUIDE = 1.5


def swapped(value, axis, bit):
    mask = 2**bit
    pairs = [(source, source ^ mask) for source in range(lax.axis_size(axis))]
    return lax.ppermute(value, axis, pairs)


def rms_scale(rows, gain):
    return rows * lax.rsqrt(jnp.mean(rows * rows, axis=-1, keepdims=True) + EPS) * gain


def split_halves(rows, is_upper, kept_count):
    lower_part = rows[:kept_count]
    upper_part = rows[kept_count:]
    outgoing = jnp.where(is_upper, lower_part, upper_part)
    own_rows = jnp.where(is_upper, upper_part, lower_part)
    return (outgoing, own_rows)


def guide_rows(own_rows, partner, is_upper):
    cond_rows = jnp.where(is_upper, partner, own_rows)
    uncond_rows = jnp.where(is_upper, own_rows, partner)
    return (uncond_rows + GUIDE * (cond_rows - uncond_rows)).astype(jnp.bfloat16)


def on_device(
    block_states,
    attn_gain,
    ffn_gain,
    final_gain,
    w_query,
    w_keyval,
    w_out,
    w_gate,
    w_up,
    w_down,
    w_head,
    cache,
    prefix_lengths,
    masked_positions,
):
    n_wide = lax.axis_size("wide")
    n_narrow = lax.axis_size("narrow")
    wide_index = lax.axis_index("wide")
    narrow_index = lax.axis_index("narrow")
    half_wide = n_wide // 2
    local_req = block_states.shape[0]
    kept_count = local_req // 2
    masked = masked_positions.shape[1]
    is_upper = wide_index >= half_wide
    full_rows = lax.all_gather(block_states, "narrow", axis=2, tiled=True)
    normed = rms_scale(full_rows.astype(jnp.float32), attn_gain).astype(jnp.bfloat16)
    kv_head = narrow_index // (n_narrow // KVH)
    head_weight = lax.dynamic_slice_in_dim(w_keyval, kv_head * (2 * HD), 2 * HD, 1)
    block_kv = jnp.einsum(
        "bld,dc->blc", normed, head_weight, preferred_element_type=jnp.float32
    ).astype(jnp.bfloat16)
    cache_kv = lax.dynamic_index_in_dim(cache, kv_head, axis=2, keepdims=False)
    first_req = wide_index % half_wide * local_req
    my_positions = lax.dynamic_slice_in_dim(masked_positions, first_req, local_req, 0)
    picked = jax.vmap(lambda rows, idx: rows[idx])(full_rows, my_positions)
    picked_normed = jax.vmap(lambda rows, idx: rows[idx])(normed, my_positions)
    local_heads = w_query.shape[1] // HD
    query = jnp.einsum(
        "bmd,dc->bmc", picked_normed, w_query, preferred_element_type=jnp.float32
    ).astype(jnp.bfloat16)
    query = query.reshape(local_req, masked, local_heads, HD)
    scale = 1.0 / math.sqrt(HD)
    pre_scores = (
        jnp.einsum("bmhd,bpd->bhmp", query, cache_kv[..., :HD], preferred_element_type=jnp.float32)
        * scale
    )
    live = jnp.arange(cache_kv.shape[1])[None, :] < prefix_lengths[:, None]
    pre_scores = jnp.where(live[:, None, None, :], pre_scores, -jnp.inf)
    blk_scores = (
        jnp.einsum("bmhd,bld->bhml", query, block_kv[..., :HD], preferred_element_type=jnp.float32)
        * scale
    )
    peak = jnp.maximum(
        jnp.max(pre_scores, axis=-1, keepdims=True), jnp.max(blk_scores, axis=-1, keepdims=True)
    )
    pre_weights = jnp.exp(pre_scores - peak)
    blk_weights = jnp.exp(blk_scores - peak)
    weight_total = jnp.sum(pre_weights, axis=-1, keepdims=True) + jnp.sum(
        blk_weights, axis=-1, keepdims=True
    )
    pre_probs = (pre_weights / weight_total).astype(jnp.bfloat16)
    blk_probs = (blk_weights / weight_total).astype(jnp.bfloat16)
    attended = jnp.einsum(
        "bhmp,bpd->bmhd", pre_probs, cache_kv[..., HD:], preferred_element_type=jnp.float32
    )
    attended = attended + jnp.einsum(
        "bhml,bld->bmhd", blk_probs, block_kv[..., HD:], preferred_element_type=jnp.float32
    )
    attended = attended.astype(jnp.bfloat16).reshape(local_req, masked, local_heads * HD)
    attn_part = jnp.einsum("bmc,cd->bmd", attended, w_out, preferred_element_type=jnp.float32)
    attn_total = lax.psum(attn_part, "narrow")
    first = picked.astype(jnp.float32) + attn_total
    ffn_in = rms_scale(first, ffn_gain).astype(jnp.bfloat16)
    gate_act = jnp.einsum("bmd,dc->bmc", ffn_in, w_gate, preferred_element_type=jnp.float32)
    up_act = jnp.einsum("bmd,dc->bmc", ffn_in, w_up, preferred_element_type=jnp.float32)
    hidden = (jax.nn.silu(gate_act) * up_act).astype(jnp.bfloat16)
    ffn_part = jnp.einsum("bmc,cd->bmd", hidden, w_down, preferred_element_type=jnp.float32)
    swap_bit = n_wide.bit_length() - 2
    vocab_cols = w_head.shape[1]
    ffn_total = lax.psum(ffn_part, "narrow")
    final = rms_scale(first + ffn_total, final_gain)
    outgoing, own_rows = split_halves(final, is_upper, kept_count)
    partner = swapped(outgoing, "wide", swap_bit)
    guided = guide_rows(own_rows, partner, is_upper).reshape(kept_count * masked, -1)
    logits = jnp.dot(
        lax.all_gather(guided, "wide", axis=0, tiled=True),
        w_head,
        preferred_element_type=jnp.float32,
    )
    logits = logits.reshape(2, half_wide, kept_count, masked, vocab_cols)
    logits = jnp.transpose(logits, (1, 0, 2, 3, 4)).reshape(-1, vocab_cols)
    local_peak = jnp.max(logits, axis=-1)
    row_peak = lax.pmax(local_peak, ("wide", "narrow"))
    row_total = lax.psum(jnp.sum(jnp.exp(logits - row_peak[:, None]), axis=-1), ("wide", "narrow"))
    lse = row_peak + jnp.log(row_total)
    log_probs = logits - lse[:, None]
    confidence = jnp.exp(row_peak - lse).reshape(-1, masked)
    return (log_probs, confidence)


def solution(mesh):
    in_specs = (
        P("wide", None, "narrow"),
        P(),
        P(),
        P(),
        P(None, "narrow"),
        P(),
        P("narrow", None),
        P(None, "narrow"),
        P(None, "narrow"),
        P("narrow", None),
        P(None, ("wide", "narrow")),
        P("wide", None, None, None),
        P("wide"),
        P(),
    )
    out_specs = (P(None, ("wide", "narrow")), P())
    return jax.shard_map(
        on_device, mesh=mesh, in_specs=in_specs, out_specs=out_specs, check_vma=False
    )
```

profile of v0, /device:TPU:1, one launch (start us, length us, event | category | flops | bytes accessed | tf_op | source)
XLA Modules:
  0.0 550.7 jit_solution(10640468757488981066)
XLA Ops:
  7.2 0.0 copy-start
  7.2 0.0 copy-start.12
  7.2 0.0 all-gather.4.cloned.1.call-start
  7.2 0.7 all-gather.4.cloned.1.call-update
  7.9 0.0 all-reduce.3.cloned.1.call-start
  8.0 0.7 fusion.54
  8.7 0.1 reshape.99
  8.8 1.1 constant_dynamic-slice_fusion
  9.9 0.1 copy.68
  10.0 0.0 copy-done.12
  10.0 0.1 iota_compare_fusion
  10.1 38.0 %all-gather.4.cloned.1.call-done = bf16[2,64,4096]{2,1,0:T(8,128)(2,1)} async-done(((bf16[2,64,512]{2,1,0:T(8,128)(2,1)}), bf16[2,64,4096]{2,1,0:T(8,128)(2,1)}) %all-gather.4.cloned.1.call-update) | async-done | bytes 1048592 | tf_op jit(solution)/shard_map/all_gather | solution.py:62
  48.1 1.5 fusion.6
  49.6 1.6 fusion.8
  51.2 3.9 gather_fusion.1
  55.0 0.0 copy-start.6
  55.1 2.2 fusion.23
  57.2 0.6 copy-done.6
  57.9 0.8 fusion.19
  58.7 0.3 fusion.58
  58.9 0.4 fusion.57
  59.3 0.1 fusion.36
  59.4 0.3 fusion.33
  59.7 0.0 copy-start.7
  59.7 0.4 fusion.35
  60.2 0.2 fusion.22
  60.4 1.5 copy-done.7
  61.9 2.1 fusion.2
  64.0 0.0 all-reduce.3.cloned.1.call-update
  64.0 0.2 all-reduce.5.cloned.1.call-start
  64.3 1.0 copy-done.2
  65.2 3.9 gather_fusion
  69.1 0.0 copy-start.10
  69.1 103.4 %all-reduce.3.cloned.1.call-done = f32[2,64,4096]{2,1,0:T(8,128)} async-done(((f32[2,64,4096]{2,1,0:T(8,128)}), f32[2,64,4096]{2,1,0:T(8,128)}) %all-reduce.3.cloned.1.call-update) | async-done | bytes 2097168 | tf_op jit(solution)/shard_map/psum | solution.py:108
  172.5 2.1 multiply_reduce_fusion.1
  174.6 0.1 copy-done.4
  174.7 1.4 multiply_convert_fusion
  176.1 1.7 fusion.31
  177.8 4.0 fusion.27
  181.8 0.0 all-reduce.5.cloned.1.call-update
  181.8 0.0 all-gather.6.cloned.1.call-start
  181.8 0.0 copy-start.11
  181.8 103.9 %all-reduce.5.cloned.1.call-done = f32[2,64,4096]{2,1,0:T(8,128)} async-done(((f32[2,64,4096]{2,1,0:T(8,128)}), f32[2,64,4096]{2,1,0:T(8,128)}) %all-reduce.5.cloned.1.call-update) | async-done | bytes 2097168 | tf_op jit(solution)/shard_map/psum | solution.py:117
  285.8 2.2 multiply_reduce_fusion
  288.0 0.6 multiply_multiply_fusion
  288.6 0.1 slice_select_fusion
  288.7 2.5 collective-permute-start
  291.2 22.3 %collective-permute-done = f32[1,64,4096]{2,1,0:T(8,128)S(1)} collective-permute-done((f32[1,64,4096]{2,1,0:T(8,128)S(1)}, f32[1,64,4096]{2,1,0:T(8,128)S(1)}, u32[]{:S(2)}, u32[]{:S(2)}) %collective-permute-start) | collective-permute-done | bytes 1048608 | tf_op jit(solution)/shard_map/ppermute | solution.py:16
  313.5 1.0 add_convert_fusion
  314.6 0.0 all-gather.6.cloned.1.call-update
  314.6 74.8 %all-gather.6.cloned.1.call-done = bf16[1,1024,4096]{2,1,0:T(8,128)(2,1)} async-done(((bf16[1,64,4096]{2,1,0:T(8,128)(2,1)}), bf16[1,1024,4096]{2,1,0:T(8,128)(2,1)}) %all-gather.6.cloned.1.call-update) | async-done | bytes 8388624 | tf_op jit(solution)/shard_map/all_gather | solution.py:123
  389.4 12.6 %fusion = f32[1024,1024]{1,0:T(8,128)S(1)} fusion(bf16[4096,1024]{1,0:T(8,128)(2,1)} %param.24, bf16[1,1024,4096]{2,1,0:T(8,128)(2,1)} %all-gather.6.cloned.1.call-done), kind=kOutput, calls=%fused_computation.2 | convolution fusion | flops 8589934592 | bytes 20971520 | tf_op jit(solution)/shard_map/dot_general | solution.py:122
  402.0 0.0 copy-start.3
  402.0 2.0 copy-done.3
  404.0 2.2 copy.39
  406.3 2.5 reduce_max.31
  408.8 0.1 reduce_max.32
  408.8 64.3 %pmax.7 = f32[1024]{0:T(1024)S(1)} all-reduce(f32[1024]{0:T(1024)S(1)} %reduce_max.32), channel_id=1, replica_groups=mesh['wide'=16,'narrow'=8] {'wide','narrow'}, use_global_device_ids=true, to_apply=%region_10.11 | all-reduce | flops 1024 | bytes 8192 | tf_op jit(solution)/shard_map/pmax | solution.py:130
  473.1 0.1 sub.51
  473.2 2.9 exponential_reduce_fusion
  476.2 0.1 reduce_sum.62
  476.2 62.5 %psum.23 = f32[1024]{0:T(1024)S(1)} all-reduce(f32[1024]{0:T(1024)S(1)} %reduce_sum.62), channel_id=1, replica_groups=mesh['wide'=16,'narrow'=8] {'wide','narrow'}, use_global_device_ids=true, to_apply=%region_12.13 | all-reduce | flops 1024 | bytes 8192 | tf_op jit(solution)/shard_map/psum | solution.py:131
  538.8 0.7 reshape.98
  539.4 4.7 bitcast_subtract_fusion
  (22 shorter events, 0.1 us)
Async XLA Ops:
  7.2 1.6 copy-start
  7.2 2.8 copy-start.12
  7.2 40.9 %all-gather.4.cloned.1.call-start = ((), (), s32[]{:S(2)}) async-start(), calls=%async_computation | async-start | bytes 1179648 | tf_op jit(solution)/shard_map/all_gather | solution.py:62
  7.9 164.6 %all-reduce.3.cloned.1.call-start = ((), (), s32[]{:S(2)}) async-start(), calls=%async_computation.1 | async-start | bytes 4194304 | tf_op jit(solution)/shard_map/psum | solution.py:108
  8.8 40.8 %copy-start.9 = (f32[4096]{0:T(1024)S(1)}, f32[4096]{0:T(1024)}, u32[]{:S(2)}) copy-start(f32[4096]{0:T(1024)} %param.15) | copy-start | bytes 49156
  55.0 2.8 copy-start.6
  59.7 2.2 copy-start.7
  64.0 1.2 copy-start.2
  64.0 221.7 %all-reduce.5.cloned.1.call-start = ((), (), s32[]{:S(2)}) async-start(), calls=%async_computation.2 | async-start | bytes 4194304 | tf_op jit(solution)/shard_map/psum | solution.py:117
  69.1 105.5 %copy-start.10 = (f32[4096]{0:T(1024)S(1)}, f32[4096]{0:T(1024)}, u32[]{:S(2)}) copy-start(f32[4096]{0:T(1024)} %param.16) | copy-start | bytes 49156
  172.5 2.2 copy-start.4
  174.7 1.4 copy-start.8
  181.8 207.7 %all-gather.6.cloned.1.call-start = ((), (), s32[]{:S(2)}) async-start(), calls=%async_computation.3 | async-start | bytes 8912896 | tf_op jit(solution)/shard_map/all_gather | solution.py:123
  181.8 106.2 %copy-start.11 = (f32[4096]{0:T(1024)S(1)}, f32[4096]{0:T(1024)}, u32[]{:S(2)}) copy-start(f32[4096]{0:T(1024)} %param.17) | copy-start | bytes 49156
  285.8 2.2 copy-start.5
  288.7 24.8 %collective-permute-start = (f32[1,64,4096]{2,1,0:T(8,128)S(1)}, f32[1,64,4096]{2,1,0:T(8,128)S(1)}, u32[]{:S(2)}, u32[]{:S(2)}) collective-permute-start(f32[1,64,4096]{2,1,0:T(8,128)S(1)} %slice_select_fusion), channel_id=1, source_target_pairs={{0,64},{8,72},{16,80},{24,88},{32,96},{40,104},{48,112},{56,120},{... | collective-permute-start | bytes 3145736 | tf_op jit(solution)/shard_map/ppermute | solution.py:16
  402.0 2.0 copy-start.3
  539.4 4.7 copy-start.1
Sparse Core Ops, SparseCore 0:
  9.6 38.3 all-gather.3
  64.1 108.3 all-reduce.2
  181.9 103.8 all-reduce.4
  314.7 74.6 all-gather.5
where the time goes:
time: 551 us
  waiting for transfers between devices  343 us (62%)
  blocking collectives  127 us (23%)
  matrix products  24.6 us (4%)
  other arithmetic  21.8 us (4%)
  local copies, waits for them, and re-layouts  17.4 us (3%)
  between operations  14 us (3%)
    psum x1, waiting for transfers between devices, on_device(): ffn_total = lax.psum(ffn_part, 'narrow')  104 us
    psum x1, waiting for transfers between devices, on_device(): attn_total = lax.psum(attn_part, 'narrow')  103 us
    all_gather x1, waiting for transfers between devices, on_device(): lax.all_gather(guided, 'wide', axis=0, tiled=True)  74.8 us
    pmax x1, blocking collectives, on_device(): row_peak = lax.pmax(local_peak, ('wide', 'narrow'))  64.3 us
    psum x1, blocking collectives, on_device(): lax.psum(jnp.sum(jnp.exp(logits - row_peak[:, None]), axis=-1), ('wide',...  62.5 us
    all_gather x1, waiting for transfers between devices, on_device(): full_rows = lax.all_gather(block_states, 'narrow', axis=2, tiled=True)  38 us
    ppermute x1, waiting for transfers between devices, swapped(): return lax.ppermute(value, axis, pairs)  22.3 us
    dot_general x1, matrix products, on_device(): jnp.dot(lax.all_gather(guided, 'wide', axis=0, tiled=True), w_head, prefe...  12.6 us
  transfers between devices with their start and end apart: 5, of which 5 were waited for; matrix products, arithmetic and copies ran while one was open for 1% of the time, Pallas kernels for 0%

commit v1 on v0

--- a/solution.py
+++ b/solution.py
@@ -59,7 +59,8 @@
     kept_count = local_req // 2
     masked = masked_positions.shape[1]
     is_upper = wide_index >= half_wide
-    full_rows = lax.all_gather(block_states, "narrow", axis=2, tiled=True)
+    parts = lax.all_gather(block_states, "narrow", axis=0, tiled=False)
+    full_rows = jnp.concatenate(parts, axis=2)
     normed = rms_scale(full_rows.astype(jnp.float32), attn_gain).astype(jnp.bfloat16)
     kv_head = narrow_index // (n_narrow // KVH)
     head_weight = lax.dynamic_slice_in_dim(w_keyval, kv_head * (2 * HD), 2 * HD, 1)

time: 551 us -> 553 us (level)
  no operation moved by 1% of the time
where the time goes in v1:
time: 553 us; the launch traced here: 552 us
  waiting for transfers between devices  343 us (62%)
  blocking collectives  127 us (23%)
  matrix products  24.5 us (4%)
  other arithmetic  21.1 us (4%)
  local copies, waits for them, and re-layouts  19.6 us (4%)
  between operations  14 us (3%)
    psum x1, waiting for transfers between devices, on_device(): attn_total = lax.psum(attn_part, 'narrow')  104 us
    psum x1, waiting for transfers between devices, on_device(): ffn_total = lax.psum(ffn_part, 'narrow')  104 us
    all_gather x1, waiting for transfers between devices, on_device(): lax.all_gather(guided, 'wide', axis=0, tiled=True)  74.8 us
    pmax x1, blocking collectives, on_device(): row_peak = lax.pmax(local_peak, ('wide', 'narrow'))  64.3 us
    psum x1, blocking collectives, on_device(): lax.psum(jnp.sum(jnp.exp(logits - row_peak[:, None]), axis=-1), ('wide',...  62.5 us
    all_gather x1, waiting for transfers between devices, on_device(): parts = lax.all_gather(block_states, 'narrow', axis=0, tiled=False)  37.2 us
    ppermute x1, waiting for transfers between devices, swapped(): return lax.ppermute(value, axis, pairs)  22.3 us
    dot_general x1, matrix products, on_device(): jnp.dot(lax.all_gather(guided, 'wide', axis=0, tiled=True), w_head, prefe...  12.6 us
  transfers between devices with their start and end apart: 5, of which 5 were waited for; matrix products, arithmetic and copies ran while one was open for 1% of the time, Pallas kernels for 0%

profile of v1, /device:TPU:1, one launch (start us, length us, event | category | flops | bytes accessed | tf_op | source)
XLA Modules:
  0.0 552.3 jit_solution(10762993623698289507)
XLA Ops:
  7.2 0.0 copy-start
  7.2 0.0 all-gather.5.cloned.1.call-start
  7.2 0.7 all-gather.5.cloned.1.call-update
  7.9 0.0 all-reduce.3.cloned.1.call-start
  8.0 0.7 fusion.51
  8.7 0.1 reshape.107
  8.8 1.1 constant_dynamic-slice_fusion
  9.9 0.9 copy.76
  10.8 0.1 iota_compare_fusion
  10.8 37.2 %all-gather.5.cloned.1.call-done = bf16[16,64,512]{2,1,0:T(8,128)(2,1)} async-done(((bf16[2,64,512]{2,1,0:T(8,128)(2,1)}), bf16[16,64,512]{2,1,0:T(8,128)(2,1)}) %all-gather.5.cloned.1.call-update) | async-done | bytes 1048592 | tf_op jit(solution)/shard_map/all_gather | solution.py:62
  48.0 2.0 multiply_reduce_fusion.2
  50.1 1.8 copy.75
  51.9 0.5 reshape.100
  52.5 0.3 multiply_convert_fusion.1
  52.8 3.9 gather_fusion.1
  56.7 0.0 copy-start.5
  56.7 2.2 fusion.20
  58.9 0.6 copy-done.5
  59.5 0.7 fusion.16
  60.2 0.3 fusion.55
  60.5 0.0 copy-done.8
  60.6 0.4 fusion.54
  61.0 0.1 fusion.33
  61.0 0.3 fusion.30
  61.4 0.0 copy-start.6
  61.4 0.4 fusion.32
  61.8 0.2 fusion.19
  62.1 1.5 copy-done.6
  63.6 2.1 fusion.2
  65.6 0.0 all-reduce.3.cloned.1.call-update
  65.7 0.2 all-reduce.5.cloned.1.call-start
  65.9 3.9 gather_fusion
  69.8 0.0 copy-start.10
  69.8 104.3 %all-reduce.3.cloned.1.call-done = f32[2,64,4096]{2,1,0:T(8,128)} async-done(((f32[2,64,4096]{2,1,0:T(8,128)}), f32[2,64,4096]{2,1,0:T(8,128)}) %all-reduce.3.cloned.1.call-update) | async-done | bytes 2097168 | tf_op jit(solution)/shard_map/psum | solution.py:109
  174.1 2.1 multiply_reduce_fusion.1
  176.3 0.1 copy-done.3
  176.3 1.4 multiply_convert_fusion
  177.7 1.7 fusion.28
  179.4 4.0 fusion.24
  183.4 0.0 all-reduce.5.cloned.1.call-update
  183.4 0.0 all-gather.7.cloned.1.call-start
  183.5 0.0 copy-start.11
  183.5 103.9 %all-reduce.5.cloned.1.call-done = f32[2,64,4096]{2,1,0:T(8,128)} async-done(((f32[2,64,4096]{2,1,0:T(8,128)}), f32[2,64,4096]{2,1,0:T(8,128)}) %all-reduce.5.cloned.1.call-update) | async-done | bytes 2097168 | tf_op jit(solution)/shard_map/psum | solution.py:118
  287.4 2.2 multiply_reduce_fusion
  289.6 0.6 multiply_multiply_fusion
  290.2 0.1 slice_select_fusion
  290.3 2.5 collective-permute-start
  292.8 22.3 %collective-permute-done = f32[1,64,4096]{2,1,0:T(8,128)S(1)} collective-permute-done((f32[1,64,4096]{2,1,0:T(8,128)S(1)}, f32[1,64,4096]{2,1,0:T(8,128)S(1)}, u32[]{:S(2)}, u32[]{:S(2)}) %collective-permute-start) | collective-permute-done | bytes 1048608 | tf_op jit(solution)/shard_map/ppermute | solution.py:16
  315.2 1.0 add_convert_fusion
  316.2 0.0 all-gather.7.cloned.1.call-update
  316.2 74.8 %all-gather.7.cloned.1.call-done = bf16[1,1024,4096]{2,1,0:T(8,128)(2,1)} async-done(((bf16[1,64,4096]{2,1,0:T(8,128)(2,1)}), bf16[1,1024,4096]{2,1,0:T(8,128)(2,1)}) %all-gather.7.cloned.1.call-update) | async-done | bytes 8388624 | tf_op jit(solution)/shard_map/all_gather | solution.py:124
  391.1 12.6 %fusion = f32[1024,1024]{1,0:T(8,128)S(1)} fusion(bf16[4096,1024]{1,0:T(8,128)(2,1)} %param.24, bf16[1,1024,4096]{2,1,0:T(8,128)(2,1)} %all-gather.7.cloned.1.call-done), kind=kOutput, calls=%fused_computation.2 | convolution fusion | flops 8589934592 | bytes 20971520 | tf_op jit(solution)/shard_map/dot_general | solution.py:123
  403.7 0.0 copy-start.2
  403.7 2.0 copy-done.2
  405.7 2.2 copy.43
  407.9 2.5 reduce_max.31
  410.4 0.1 reduce_max.32
  410.5 64.3 %pmax.7 = f32[1024]{0:T(1024)S(1)} all-reduce(f32[1024]{0:T(1024)S(1)} %reduce_max.32), channel_id=1, replica_groups=mesh['wide'=16,'narrow'=8] {'wide','narrow'}, use_global_device_ids=true, to_apply=%region_10.11 | all-reduce | flops 1024 | bytes 8192 | tf_op jit(solution)/shard_map/pmax | solution.py:131
  474.8 0.1 sub.51
  474.9 2.9 exponential_reduce_fusion
  477.8 0.1 reduce_sum.62
  477.9 62.5 %psum.23 = f32[1024]{0:T(1024)S(1)} all-reduce(f32[1024]{0:T(1024)S(1)} %reduce_sum.62), channel_id=1, replica_groups=mesh['wide'=16,'narrow'=8] {'wide','narrow'}, use_global_device_ids=true, to_apply=%region_12.13 | all-reduce | flops 1024 | bytes 8192 | tf_op jit(solution)/shard_map/psum | solution.py:132
  540.4 0.7 reshape.106
  541.1 4.7 bitcast_subtract_fusion
  (24 shorter events, 0.1 us)
Async XLA Ops:
  7.2 1.6 copy-start
  7.2 3.6 copy-start.12
  7.2 40.9 %all-gather.5.cloned.1.call-start = ((), (), s32[]{:S(2)}) async-start(), calls=%async_computation.2 | async-start | bytes 1179648 | tf_op jit(solution)/shard_map/all_gather | solution.py:62
  7.9 166.2 %all-reduce.3.cloned.1.call-start = ((), (), s32[]{:S(2)}) async-start(), calls=%async_computation | async-start | bytes 4194304 | tf_op jit(solution)/shard_map/psum | solution.py:109
  50.1 2.4 copy-start.9
  56.7 2.8 copy-start.5
  59.5 1.0 copy-start.8
  61.4 2.2 copy-start.6
  65.7 221.7 %all-reduce.5.cloned.1.call-start = ((), (), s32[]{:S(2)}) async-start(), calls=%async_computation.1 | async-start | bytes 4194304 | tf_op jit(solution)/shard_map/psum | solution.py:118
  69.8 106.5 %copy-start.10 = (f32[4096]{0:T(1024)S(1)}, f32[4096]{0:T(1024)}, u32[]{:S(2)}) copy-start(f32[4096]{0:T(1024)} %param.16) | copy-start | bytes 49156
  174.1 2.2 copy-start.3
  176.3 1.4 copy-start.7
  183.4 207.6 %all-gather.7.cloned.1.call-start = ((), (), s32[]{:S(2)}) async-start(), calls=%async_computation.3 | async-start | bytes 8912896 | tf_op jit(solution)/shard_map/all_gather | solution.py:124
  183.5 106.2 %copy-start.11 = (f32[4096]{0:T(1024)S(1)}, f32[4096]{0:T(1024)}, u32[]{:S(2)}) copy-start(f32[4096]{0:T(1024)} %param.17) | copy-start | bytes 49156
  287.4 2.2 copy-start.4
  290.3 24.8 %collective-permute-start = (f32[1,64,4096]{2,1,0:T(8,128)S(1)}, f32[1,64,4096]{2,1,0:T(8,128)S(1)}, u32[]{:S(2)}, u32[]{:S(2)}) collective-permute-start(f32[1,64,4096]{2,1,0:T(8,128)S(1)} %slice_select_fusion), channel_id=1, source_target_pairs={{0,64},{8,72},{16,80},{24,88},{32,96},{40,104},{48,112},{56,120},{... | collective-permute-start | bytes 3145736 | tf_op jit(solution)/shard_map/ppermute | solution.py:16
  403.7 2.0 copy-start.2
  541.1 4.7 copy-start.1
Sparse Core Ops, SparseCore 0:
  9.6 38.3 all-gather.4
  65.8 108.2 all-reduce.2
  183.5 103.8 all-reduce.4
  316.4 74.6 all-gather.6
